TPU v7x, 32 devices: a whole 2x2x4 slice. The times are simulated.
32 devices in a mesh: rows: 4 (over x, core), labels: 8 (over z, y).
Axes of the slice: x: 2, y: 2, z: 4, core: 2. Of those that a mesh axis runs over, the one named last changes fastest.
Arguments:
- pool_features: bfloat16 [512, 768], P('rows'), may hold values from -6 to 6
- pool_labels: int32 [512, 16], P('rows'), may hold values from 0 to 12287
- pool_counts: int32 [512], P('rows'), may hold values from 1 to 16
- batch_rows: int32 [2, 128], P(None, 'rows'), may hold values from 0 to 127
- weights: float32 [12288, 768], P(('rows', 'labels')), may hold values from -0.21875 to 0.21875
- momentum: float32 [12288, 768], P(('rows', 'labels')), may hold values from -24 to 24
Outputs:
- new_weights: float32 [12288, 768], P(('rows', 'labels'))
- new_momentum: float32 [12288, 768], P(('rows', 'labels'))
- feature_grads: float32 [2, 128, 768], P(None, 'rows')
Inputs may be any that keep to these rules, and one draw needn't show every extreme that they name: `pool_labels`: slots of a list at or past its count are padding and are ignored; a label may appear twice in a list. `batch_rows`: an entry names one of the 128 examples stored with the index of rows that owns that batch row.
All inputs are finite; a program needn't handle non-finite values.
Results may differ from a plain program's by a relative error of at most 0.00045.
The roundings to bfloat16 on the way count: a program that leaves them out, or rounds other values in their place, can miss the bound.
Values may be sent and summed in bfloat16 or wider, within the bound.
No kernel may reach another device: no remote copies, remote signals or barrier semaphores. Data moves between devices by JAX's collectives and lax.ppermute only.
A program may use at most 64 MiB of HBM per device.

v0:
```python
import jax
import jax.numpy as jnp
from jax import lax
from jax.sharding import PartitionSpec as P

learn_rate = 0.001
decay_rate = 0.9


def feature_sums(errors_list, lowered_list, width):
    parts = []
    for errors, low_weights in zip(errors_list, lowered_list):
        parts.append(jnp.dot(errors, low_weights, preferred_element_type=jnp.float32))
    grouped = lax.psum_scatter(
        jnp.concatenate(parts, axis=1), "rows", scatter_dimension=0, tiled=True
    )
    mine = lax.psum(grouped, "labels")
    return jnp.stack([mine[:, :width], mine[:, width:]])


def per_device(pool_features, pool_labels, pool_counts, batch_rows, weights, momentum):
    lab_rows = weights.shape[0]
    width = weights.shape[1]
    device_index = lax.axis_index("rows") * lax.axis_size("labels") + lax.axis_index("labels")
    labels = device_index * lab_rows + jnp.arange(lab_rows, dtype=jnp.int32)
    all_ids, all_counts = (
        lax.all_gather(pool_labels[batch_rows], "rows", axis=1, tiled=True),
        lax.all_gather(pool_counts[batch_rows], "rows", axis=1, tiled=True),
    )
    all_features = lax.all_gather(pool_features[batch_rows], "rows", axis=1, tiled=True)
    errors_list = []
    lowered_list = []
    for batch in range(2):
        features = all_features[batch]
        label_ids = all_ids[batch]
        in_list = (
            jnp.arange(label_ids.shape[1], dtype=jnp.int32)[None, :] < all_counts[batch][:, None]
        )
        matched = (label_ids[:, :, None] == labels[None, None, :]) & in_list[:, :, None]
        targets = jnp.any(matched, axis=1).astype(jnp.float32)
        low_weights = weights.astype(jnp.bfloat16)
        logits = lax.dot_general(
            features, low_weights, (((1,), (1,)), ((), ())), preferred_element_type=jnp.float32
        )
        errors = (jax.nn.sigmoid(logits) - targets).astype(jnp.bfloat16)
        grads = lax.dot_general(
            errors, features, (((0,), (0,)), ((), ())), preferred_element_type=jnp.float32
        )
        errors_list.append(errors)
        lowered_list.append(low_weights)
        momentum = decay_rate * momentum + grads
        weights = weights - learn_rate * momentum
    return (weights, momentum, feature_sums(errors_list, lowered_list, width))


def solution(mesh):
    in_specs = (
        P("rows", None),
        P("rows", None),
        P("rows"),
        P(None, "rows"),
        P(("rows", "labels"), None),
        P(("rows", "labels"), None),
    )
    out_specs = (P(("rows", "labels"), None), P(("rows", "labels"), None), P(None, "rows", None))
    return jax.shard_map(
        per_device, mesh=mesh, in_specs=in_specs, out_specs=out_specs, check_vma=False
    )
```

profile of v0, /device:TPU:0, one launch (start us, length us, event | category | flops | bytes accessed | tf_op | source)
XLA Modules:
  0.0 143.2 jit_solution(4166280901989840444)
XLA Ops:
  7.2 0.0 copy-start
  7.2 0.0 reduce-scatter.2.cloned.1.call-start
  7.2 0.7 compare_select_fusion
  7.9 0.1 reshape.62
  8.0 1.4 gather_fusion.2
  9.5 0.1 reshape.81
  9.6 6.0 %all-gather.3 = s32[4,32,2]{1,2,0:T(2,128)S(1)} all-gather(s32[1,32,2]{1,2,0:T(2,128)S(1)} %bitcast.41), channel_id=4, replica_groups=mesh['rows'=4,'labels'=8] {'rows'}, dimensions={0}, use_global_device_ids=true | all-gather | bytes 1280 | tf_op jit(solution)/shard_map/all_gather | solution.py:28
  15.6 0.1 reshape.94
  15.7 0.8 copy.14
  16.5 0.6 gather_fusion.1
  17.1 0.0 copy-done
  17.1 0.7 gather_fusion
  17.8 5.7 %all-gather.1 = s32[2,128,16]{2,1,0:T(8,128)S(1)} all-gather(s32[2,32,16]{2,1,0:T(8,128)S(1)} %bitcast.39), channel_id=3, replica_groups=mesh['rows'=4,'labels'=8] {'rows'}, dimensions={1}, use_global_device_ids=true | all-gather | bytes 20480 | tf_op jit(solution)/shard_map/all_gather | solution.py:27
  23.5 6.7 %all-gather = bf16[2,128,768]{2,1,0:T(8,128)(2,1)S(1)} all-gather(bf16[2,32,768]{2,1,0:T(8,128)(2,1)S(1)} %bitcast.38), channel_id=2, replica_groups=mesh['rows'=4,'labels'=8] {'rows'}, dimensions={1}, use_global_device_ids=true | all-gather | bytes 491520 | tf_op jit(solution)/shard_map/all_gather | solution.py:30
  30.2 0.1 iota_compare_fusion
  30.3 2.0 %and_reduce_fusion = (pred[128,384]{1,0:T(8,128)(4,1)S(1)}, pred[128,384]{1,0:T(8,128)(4,1)S(1)}) fusion(s32[128,16]{1,0:T(8,128)S(1)} %get-tuple-element.8, s32[384]{0:T(512)S(1)} %iota_add_fusion, pred[128,16]{1,0:T(8,128)(4,1)S(1)} %get-tuple-element.15, pred[128,16]{1,0:T(8,128)(4,1)S(1)} %get-tuple-element.16, s32[128,16]{1,0:T(8,128)S(1)} %get-tuple-element.7), kind=kLoop, calls=%fused_computation.3 | loop fusion | flops 4620288 | bytes 120320 | tf_op jit(solution)/shard_map/reduce_or | solution.py:40
  32.4 0.3 fusion.9
  32.7 0.0 copy-start.2
  32.7 0.3 fusion.11
  33.0 1.0 copy-done.2
  34.0 0.4 fusion.10
  34.4 0.3 fusion.8
  34.7 0.3 fusion.14
  35.0 1.0 pad_maximum_fusion
  36.0 0.0 reduce-scatter.2.cloned.1.call-update
  36.0 0.0 all-reduce.2.cloned.1.call-start
  36.0 24.7 %reduce-scatter.2.cloned.1.call-done = f32[32,1536]{1,0:T(8,128)} async-done(((f32[128,1536]{1,0:T(8,128)}), f32[32,1536]{1,0:T(8,128)}) %reduce-scatter.2.cloned.1.call-update) | async-done | bytes 196624 | tf_op jit(solution)/shard_map/reduce_scatter | solution.py:14
  60.7 0.0 all-reduce.2.cloned.1.call-update
  60.7 1.9 %multiply_subtract_fusion = (f32[384,768]{1,0:T(8,128)}, f32[384,768]{1,0:T(8,128)}) fusion(f32[384,768]{1,0:T(8,128)S(1)} %copy-done.1, f32[384,768]{1,0:T(8,128)S(1)} %get-tuple-element.12, bf16[128,384]{1,0:T(8,128)(2,1)S(1)} %fusion.8, bf16[2,128,768]{2,1,0:T(8,128)(2,1)S(1)} %all-gather), kind=kOutput, calls=%fused_computation.7 | convolution fusion | flops 77266944 | bytes 5013504 | tf_op jit(solution)/shard_map/dot_general | solution.py:46
  62.6 72.1 %all-reduce.2.cloned.1.call-done = f32[32,1536]{1,0:T(8,128)} async-done(((f32[32,1536]{1,0:T(8,128)}), f32[32,1536]{1,0:T(8,128)}) %all-reduce.2.cloned.1.call-update) | async-done | bytes 196624 | tf_op jit(solution)/shard_map/psum | solution.py:17
  134.7 1.0 slice_bitcast_fusion.7
  135.6 0.7 pad_maximum_fusion.1
  (7 shorter events, 0.0 us)
Async XLA Ops:
  7.2 9.9 %copy-start = (bf16[128,768]{1,0:T(8,128)(2,1)S(1)}, bf16[128,768]{1,0:T(8,128)(2,1)}, u32[]{:S(2)}) copy-start(bf16[128,768]{1,0:T(8,128)(2,1)} %param.6) | copy-start | bytes 589828
  7.2 53.5 %reduce-scatter.2.cloned.1.call-start = ((), (), s32[]{:S(2)}) async-start(), calls=%async_computation.1 | async-start | bytes 983040 | tf_op jit(solution)/shard_map/reduce_scatter | solution.py:14
  16.5 15.9 %copy-start.1 = (f32[384,768]{1,0:T(8,128)S(1)}, f32[384,768]{1,0:T(8,128)}, u32[]{:S(2)}) copy-start(f32[384,768]{1,0:T(8,128)} %param.10) | copy-start | bytes 3538948
  32.7 1.3 copy-start.2
  36.0 98.7 %all-reduce.2.cloned.1.call-start = ((), (), s32[]{:S(2)}) async-start(), calls=%async_computation.2 | async-start | bytes 393216 | tf_op jit(solution)/shard_map/psum | solution.py:17
Sparse Core Ops, SparseCore 0:
  36.1 24.5 reduce-scatter.1
  64.0 70.6 all-reduce.1
where the time goes:
time: 143 us
  waiting for transfers between devices  96.8 us (68%)
  blocking collectives  18.4 us (13%)
  between operations  14.1 us (10%)
  local copies, waits for them, and re-layouts  5.77 us (4%)
  other arithmetic  4.51 us (3%)
  matrix products  3.49 us (2%)
    psum x1, waiting for transfers between devices, feature_sums(): mine = lax.psum(grouped, 'labels')  72.1 us
    reduce_scatter x1, waiting for transfers between devices, feature_sums(): lax.psum_scatter(jnp.concatenate(parts, axis=1), 'rows', scatter_dimensio...  24.7 us
    all_gather x1, blocking collectives, per_device(): lax.all_gather(pool_features[batch_rows], 'rows', axis=1, tiled=True)  6.67 us
    all_gather x1, blocking collectives, per_device(): lax.all_gather(pool_counts[batch_rows], 'rows', axis=1, tiled=True)  6.01 us
    all_gather x1, blocking collectives, per_device(): lax.all_gather(pool_labels[batch_rows], 'rows', axis=1, tiled=True)  5.73 us
  transfers between devices with their start and end apart: 2, of which 2 were waited for; matrix products, arithmetic and copies ran while one was open for 1% of the time, Pallas kernels for 0%

commit v1 on v0

--- a/solution.py
+++ b/solution.py
@@ -14,7 +14,7 @@
     grouped = lax.psum_scatter(
         jnp.concatenate(parts, axis=1), "rows", scatter_dimension=0, tiled=True
     )
-    mine = lax.psum(grouped, "labels")
+    mine = jnp.sum(lax.all_gather(grouped, "labels"), axis=0)
     return jnp.stack([mine[:, :width], mine[:, width:]])
 
 

time: 143 us -> 116 us (0.81)
  waiting for transfers between devices: 96.8 us -> 69.2 us
  other arithmetic: 4.51 us -> 6.02 us
    psum x1 -> x0, waiting for transfers between devices: 72.1 us -> none  [feature_sums(): mine = lax.psum(grouped, 'labels')]
    all_gather x0 -> x1, waiting for transfers between devices: none -> 44.5 us  [feature_sums(): mine = jnp.sum(lax.all_gather(grouped, 'labels'), axis=0)]
    reduce_sum x0 -> x1, other arithmetic: none -> 1.51 us  [feature_sums(): mine = jnp.sum(lax.all_gather(grouped, 'labels'), axis=0)]
  transfers between devices with their start and end apart: 2 -> 2, of which waited for: 2 -> 2; matrix products, arithmetic and copies ran while one was open for 1% -> 2% of each run, Pallas kernels for 0% -> 0%
where the time goes in v1:
time: 116 us
  waiting for transfers between devices  69.2 us (60%)
  blocking collectives  18.4 us (16%)
  between operations  14.1 us (12%)
  other arithmetic  6.02 us (5%)
  local copies, waits for them, and re-layouts  4.83 us (4%)
  matrix products  3.49 us (3%)
    all_gather x1, waiting for transfers between devices, feature_sums(): mine = jnp.sum(lax.all_gather(grouped, 'labels'), axis=0)  44.5 us
    reduce_scatter x1, waiting for transfers between devices, feature_sums(): lax.psum_scatter(jnp.concatenate(parts, axis=1), 'rows', scatter_dimensio...  24.7 us
    all_gather x1, blocking collectives, per_device(): lax.all_gather(pool_features[batch_rows], 'rows', axis=1, tiled=True)  6.67 us
    all_gather x1, blocking collectives, per_device(): lax.all_gather(pool_counts[batch_rows], 'rows', axis=1, tiled=True)  6.01 us
    all_gather x1, blocking collectives, per_device(): lax.all_gather(pool_labels[batch_rows], 'rows', axis=1, tiled=True)  5.73 us
  transfers between devices with their start and end apart: 2, of which 2 were waited for; matrix products, arithmetic and copies ran while one was open for 2% of the time, Pallas kernels for 0%

profile of v1, /device:TPU:0, one launch (start us, length us, event | category | flops | bytes accessed | tf_op | source)
XLA Modules:
  0.0 116.2 jit_solution(13316181050092365854)
XLA Ops:
  7.2 0.0 copy-start
  7.2 0.0 reduce-scatter.2.cloned.1.call-start
  7.2 0.7 compare_select_fusion
  7.9 0.1 reshape.62
  8.0 1.4 %gather_fusion.2 = s32[64]{0:T(128)S(1)} fusion(s32[128]{0:T(128)} %param.8, s32[1024]{0:T(1024)S(1)} %pad_clamp_fusion), kind=kCustom, calls=%fused_computation.2 | custom fusion | bytes 768 | tf_op jit(solution)/shard_map/gather | solution.py:28
  9.5 0.1 reshape.81
  9.6 6.0 %all-gather.4 = s32[4,32,2]{1,2,0:T(2,128)S(1)} all-gather(s32[1,32,2]{1,2,0:T(2,128)S(1)} %bitcast.43), channel_id=4, replica_groups=mesh['rows'=4,'labels'=8] {'rows'}, dimensions={0}, use_global_device_ids=true | all-gather | bytes 1280 | tf_op jit(solution)/shard_map/all_gather | solution.py:28
  15.6 0.1 reshape.95
  15.7 0.8 copy.14
  16.5 0.6 gather_fusion.1
  17.1 0.0 copy-done
  17.1 0.7 gather_fusion
  17.8 5.7 %all-gather.1 = s32[2,128,16]{2,1,0:T(8,128)S(1)} all-gather(s32[2,32,16]{2,1,0:T(8,128)S(1)} %bitcast.41), channel_id=3, replica_groups=mesh['rows'=4,'labels'=8] {'rows'}, dimensions={1}, use_global_device_ids=true | all-gather | bytes 20480 | tf_op jit(solution)/shard_map/all_gather | solution.py:27
  23.5 6.7 %all-gather = bf16[2,128,768]{2,1,0:T(8,128)(2,1)S(1)} all-gather(bf16[2,32,768]{2,1,0:T(8,128)(2,1)S(1)} %bitcast.40), channel_id=2, replica_groups=mesh['rows'=4,'labels'=8] {'rows'}, dimensions={1}, use_global_device_ids=true | all-gather | bytes 491520 | tf_op jit(solution)/shard_map/all_gather | solution.py:30
  30.2 0.1 iota_compare_fusion
  30.3 2.0 %and_reduce_fusion = (pred[128,384]{1,0:T(8,128)(4,1)S(1)}, pred[128,384]{1,0:T(8,128)(4,1)S(1)}) fusion(s32[128,16]{1,0:T(8,128)S(1)} %get-tuple-element.8, s32[384]{0:T(512)S(1)} %iota_add_fusion, pred[128,16]{1,0:T(8,128)(4,1)S(1)} %get-tuple-element.15, pred[128,16]{1,0:T(8,128)(4,1)S(1)} %get-tuple-element.16, s32[128,16]{1,0:T(8,128)S(1)} %get-tuple-element.7), kind=kLoop, calls=%fused_computation.3 | loop fusion | flops 4620288 | bytes 120320 | tf_op jit(solution)/shard_map/reduce_or | solution.py:40
  32.4 0.3 fusion.9
  32.7 0.0 copy-start.2
  32.7 0.3 fusion.11
  33.0 1.0 copy-done.2
  34.0 0.4 fusion.10
  34.4 0.3 fusion.8
  34.7 0.3 fusion.14
  35.0 1.0 pad_maximum_fusion
  36.0 0.0 reduce-scatter.2.cloned.1.call-update
  36.0 0.0 all-gather.7.cloned.1.call-start
  36.0 24.7 %reduce-scatter.2.cloned.1.call-done = f32[32,1536]{1,0:T(8,128)} async-done(((f32[128,1536]{1,0:T(8,128)}), f32[32,1536]{1,0:T(8,128)}) %reduce-scatter.2.cloned.1.call-update) | async-done | bytes 196624 | tf_op jit(solution)/shard_map/reduce_scatter | solution.py:14
  60.7 0.0 all-gather.7.cloned.1.call-update
  60.7 1.9 %multiply_subtract_fusion = (f32[384,768]{1,0:T(8,128)}, f32[384,768]{1,0:T(8,128)}) fusion(f32[384,768]{1,0:T(8,128)S(1)} %copy-done.1, f32[384,768]{1,0:T(8,128)S(1)} %get-tuple-element.12, bf16[128,384]{1,0:T(8,128)(2,1)S(1)} %fusion.8, bf16[2,128,768]{2,1,0:T(8,128)(2,1)S(1)} %all-gather), kind=kOutput, calls=%fused_computation.7 | convolution fusion | flops 77266944 | bytes 5013504 | tf_op jit(solution)/shard_map/dot_general | solution.py:46
  62.6 44.5 %all-gather.7.cloned.1.call-done = f32[256,1536]{1,0:T(8,128)} async-done(((f32[32,1536]{1,0:T(8,128)}), f32[256,1536]{1,0:T(8,128)}) %all-gather.7.cloned.1.call-update) | async-done | bytes 1572880 | tf_op jit(solution)/shard_map/all_gather | solution.py:17
  107.1 1.5 %reduce_sum.9 = f32[32,1536]{1,0:T(8,128)S(1)} reduce(f32[8,32,1536]{2,1,0:T(8,128)} %bitcast.39, f32[]{:T(128)} %constant.25.clone.1), dimensions={0}, to_apply=%region_3.0 | reduce | flops 344064 | bytes 1769476 | tf_op jit(solution)/shard_map/reduce_sum | solution.py:17
  108.6 0.7 pad_maximum_fusion.1
  (8 shorter events, 0.0 us)
Async XLA Ops:
  7.2 9.9 %copy-start = (bf16[128,768]{1,0:T(8,128)(2,1)S(1)}, bf16[128,768]{1,0:T(8,128)(2,1)}, u32[]{:S(2)}) copy-start(bf16[128,768]{1,0:T(8,128)(2,1)} %param.6) | copy-start | bytes 589828
  7.2 53.5 %reduce-scatter.2.cloned.1.call-start = ((), (), s32[]{:S(2)}) async-start(), calls=%async_computation.1 | async-start | bytes 983040 | tf_op jit(solution)/shard_map/reduce_scatter | solution.py:14
  16.5 15.9 %copy-start.1 = (f32[384,768]{1,0:T(8,128)S(1)}, f32[384,768]{1,0:T(8,128)}, u32[]{:S(2)}) copy-start(f32[384,768]{1,0:T(8,128)} %param.10) | copy-start | bytes 3538948
  32.7 1.3 %copy-start.2 = (f32[384,768]{1,0:T(8,128)S(1)}, f32[384,768]{1,0:T(8,128)}, u32[]{:S(2)}) copy-start(f32[384,768]{1,0:T(8,128)} %param.11) | copy-start | bytes 3538948
  36.0 71.1 %all-gather.7.cloned.1.call-start = ((), (), s32[]{:S(2)}) async-start(), calls=%async_computation.2 | async-start | bytes 1769472 | tf_op jit(solution)/shard_map/all_gather | solution.py:17
Sparse Core Ops, SparseCore 0:
  36.1 24.5 reduce-scatter.1
  62.9 44.1 all-gather.6
